TPU v7x, 768 devices: a whole 4x8x12 slice. The times are simulated.
768 devices in a mesh: adapter: 24 (over z, core), tensor: 32 (over y, x).
Axes of the slice: x: 4, y: 8, z: 12, core: 2. Of those that a mesh axis runs over, the one named last changes fastest.
Arguments:
- rollout_activations: bfloat16 [6144, 8192], P('adapter'), may hold values from -6 to 6
- projection_weight: bfloat16 [8192, 8192], P(None, 'tensor'), may hold values from -0.0625 to 0.0625
- adapter_down_panels: bfloat16 [384, 64, 8192], P('adapter', None, 'tensor'), may hold values from -0.0625 to 0.0625
- adapter_up_panels: bfloat16 [384, 64, 8192], P('adapter', None, 'tensor'), may hold values from -0.75 to 0.75
- output_gradient: bfloat16 [6144, 8192], P('adapter', 'tensor'), may hold values from -1.5 to 1.5
- segment_adapter: int32 [48], replicated, may hold values from 0 to 383, as said below
Outputs:
- projection_output: bfloat16 [6144, 8192], P('adapter', 'tensor')
- gradient_of_input: bfloat16 [6144, 8192], P('adapter', 'tensor')
- down_grad: bfloat16 [384, 64, 8192], P('adapter', None, 'tensor')
- up_grad: bfloat16 [384, 64, 8192], P('adapter', None, 'tensor')
Inputs may be any that keep to these rules, and one draw needn't show every extreme that they name: `segment_adapter`: among the adapters of one owner, o * 16 to (o + 1) * 16 - 1, at most 2 distinct ones are named; some owner has exactly 2 named, and some segment names adapter 384 - 1.
All inputs are finite; a program needn't handle non-finite values.
Results may differ from a plain program's by a relative error of at most 0.02.
Values may be sent and summed in bfloat16 or wider, within the bound.
A program may use at most 64 MiB of HBM per device.

v0:
```python
import jax
import jax.numpy as jnp
from jax import lax
from jax.sharding import PartitionSpec as P

SEG_ROWS = 128
ADP_OWN = 16
ACTIVE = 2


adapter_scale = 0.5


def per_device(
    rollout_activations,
    projection_weight,
    adapter_down_panels,
    adapter_up_panels,
    output_gradient,
    segment_adapter,
):
    owners = lax.axis_size("adapter")
    group_pos = lax.axis_index("adapter")
    tensor_pos = lax.axis_index("tensor")
    col_width = projection_weight.shape[1]
    row_count = rollout_activations.shape[0]
    seg_count = row_count // SEG_ROWS
    group_ids = lax.dynamic_slice_in_dim(segment_adapter, group_pos * seg_count, seg_count)
    group_owner = group_ids // ADP_OWN
    acts_cols = lax.dynamic_slice_in_dim(rollout_activations, tensor_pos * col_width, col_width, 1)
    rows_cols = acts_cols.reshape(seg_count, SEG_ROWS, col_width)
    grad_cols = output_gradient.reshape(seg_count, SEG_ROWS, col_width)
    all_ids = jnp.arange(owners * ADP_OWN, dtype=jnp.int32)
    in_use = jnp.any(segment_adapter[:, None] == all_ids[None, :], axis=0)
    use_grid = in_use.reshape(owners, ADP_OWN).astype(jnp.int32)
    slot_rank = jnp.cumsum(use_grid, axis=1) - 1
    group_slots = group_owner * ACTIVE + slot_rank.reshape(-1)[group_ids]
    seg_onehot = group_slots[:, None] == jnp.arange(owners * ACTIVE, dtype=jnp.int32)[None, :]
    own_use = lax.dynamic_index_in_dim(use_grid, group_pos, 0, keepdims=False)
    own_rank = lax.dynamic_index_in_dim(slot_rank, group_pos, 0, keepdims=False)
    picker = (own_rank[None, :] == jnp.arange(ACTIVE, dtype=jnp.int32)[:, None]) & (
        own_use[None, :] > 0
    )
    selector_halfprec = picker.astype(jnp.bfloat16)
    packed_down = jnp.einsum(
        "zn,nxm->zxm", selector_halfprec, adapter_down_panels, preferred_element_type=jnp.float32
    ).astype(jnp.bfloat16)
    packed_up = jnp.einsum(
        "zn,nxm->zxm", selector_halfprec, adapter_up_panels, preferred_element_type=jnp.float32
    ).astype(jnp.bfloat16)
    gathered_down, gathered_up = (
        lax.all_gather(packed_down, "adapter", axis=0, tiled=True),
        lax.all_gather(packed_up, "adapter", axis=0, tiled=True),
    )
    onehot_half = seg_onehot.astype(jnp.bfloat16)
    seg_down = jnp.einsum(
        "sa,akd->skd", onehot_half, gathered_down, preferred_element_type=jnp.float32
    ).astype(jnp.bfloat16)
    seg_up = jnp.einsum(
        "sa,akd->skd", onehot_half, gathered_up, preferred_element_type=jnp.float32
    ).astype(jnp.bfloat16)
    down_part = jnp.einsum("srd,skd->srk", rows_cols, seg_down, preferred_element_type=jnp.float32)
    back_part = jnp.einsum("srd,skd->srk", grad_cols, seg_up, preferred_element_type=jnp.float32)
    low_rank = lax.psum(down_part.astype(jnp.bfloat16), "tensor")
    frozen_output = jnp.dot(
        rollout_activations, projection_weight, preferred_element_type=jnp.float32
    )
    adapter_output = jnp.einsum(
        "ghi,gip->ghp", low_rank, seg_up, preferred_element_type=jnp.float32
    ).reshape(row_count, col_width)
    projection_output = (frozen_output + adapter_scale * adapter_output).astype(jnp.bfloat16)
    backward_rank_terms = lax.psum(back_part.astype(jnp.bfloat16), "tensor").astype(jnp.float32)
    backward_halfprec = (adapter_scale * backward_rank_terms).astype(jnp.bfloat16)
    frozen_backward = lax.psum_scatter(
        lax.dot_general(
            projection_weight,
            output_gradient,
            (((1,), (1,)), ((), ())),
            preferred_element_type=jnp.float32,
        ).astype(jnp.bfloat16),
        "tensor",
        scatter_dimension=0,
        tiled=True,
    ).astype(jnp.float32)
    adapter_backward = jnp.einsum(
        "ghi,gip->ghp", backward_halfprec, seg_down, preferred_element_type=jnp.float32
    ).reshape(row_count, col_width)
    gradient_of_input = (frozen_backward.T + adapter_backward).astype(jnp.bfloat16)
    down_terms = jnp.einsum(
        "iap,iaj->ipj", backward_halfprec, rows_cols, preferred_element_type=jnp.float32
    )
    upward_terms = adapter_scale * jnp.einsum(
        "iap,iaj->ipj", low_rank, grad_cols, preferred_element_type=jnp.float32
    )
    onehot_float = seg_onehot.astype(jnp.float32)
    slot_down = jnp.einsum("sa,skd->akd", onehot_float, down_terms).astype(jnp.bfloat16)
    slot_up = jnp.einsum("sa,skd->akd", onehot_float, upward_terms).astype(jnp.bfloat16)
    owned_down, owned_up = (
        lax.psum_scatter(slot_down, "adapter", scatter_dimension=0, tiled=True).astype(jnp.float32),
        lax.psum_scatter(slot_up, "adapter", scatter_dimension=0, tiled=True).astype(jnp.float32),
    )
    picker_float = picker.astype(jnp.float32)
    down_grad = jnp.einsum("al,akd->lkd", picker_float, owned_down).astype(jnp.bfloat16)
    up_grad = jnp.einsum("al,akd->lkd", picker_float, owned_up).astype(jnp.bfloat16)
    return (projection_output, gradient_of_input, down_grad, up_grad)


def solution(mesh):
    in_specs = (
        P("adapter", None),
        P(None, "tensor"),
        P("adapter", None, "tensor"),
        P("adapter", None, "tensor"),
        P("adapter", "tensor"),
        P(),
    )
    out_specs = (
        P("adapter", "tensor"),
        P("adapter", "tensor"),
        P("adapter", None, "tensor"),
        P("adapter", None, "tensor"),
    )
    return jax.shard_map(
        per_device, mesh=mesh, in_specs=in_specs, out_specs=out_specs, check_vma=False
    )
```

profile of v0, /device:TPU:1, one launch (start us, length us, event | category | flops | bytes accessed | tf_op | source)
XLA Modules:
  0.0 717.3 jit_solution(17191558113932466532)
XLA Ops:
  7.2 0.0 copy-start
  7.2 0.0 copy-start.4
  7.2 0.0 all-gather.3.cloned.1.call-start
  7.2 0.8 fusion.17
  8.1 0.1 reshape.32
  8.1 0.2 reduce_window_sum.11
  8.4 0.0 copy-done
  8.4 0.4 convolution_convert_fusion.6
  8.8 0.6 copy.47
  9.4 0.0 all-gather.3.cloned.1.call-update
  9.4 0.0 all-gather.5.cloned.1.call-start
  9.5 1.4 convolution_convert_fusion.5
  10.9 0.6 copy.51
  11.6 0.0 all-gather.5.cloned.1.call-update
  11.6 0.0 all-reduce.3.cloned.1.call-start
  11.6 0.1 sub.12
  11.7 0.0 copy-done.4
  11.7 0.1 compare_select_fusion
  11.8 0.6 gather_fusion
  12.4 0.9 constant_dynamic-slice_fusion.2
  13.4 0.1 multiply_add_fusion
  13.4 0.0 copy-start.1
  13.4 65.5 %all-gather.3.cloned.1.call-done = bf16[48,64,256]{2,1,0:T(8,128)(2,1)} async-done(((bf16[2,64,256]{2,1,0:T(8,128)(2,1)}), bf16[48,64,256]{2,1,0:T(8,128)(2,1)}) %all-gather.3.cloned.1.call-update) | async-done | bytes 1572880 | tf_op jit(solution)/shard_map/all_gather | solution.py:52
  78.9 2.4 fusion.5
  81.3 0.8 convolution_convert_fusion.8
  82.1 56.6 %all-gather.5.cloned.1.call-done = bf16[48,64,256]{2,1,0:T(8,128)(2,1)} async-done(((bf16[2,64,256]{2,1,0:T(8,128)(2,1)}), bf16[48,64,256]{2,1,0:T(8,128)(2,1)}) %all-gather.5.cloned.1.call-update) | async-done | bytes 1572880 | tf_op jit(solution)/shard_map/all_gather | solution.py:53
  138.7 2.4 fusion.8
  141.1 0.0 copy-done.1
  141.1 0.8 fusion.11
  141.9 0.0 all-reduce.3.cloned.1.call-update
  141.9 0.0 reduce-scatter.6.cloned.1.call-start
  141.9 154.5 %all-reduce.3.cloned.1.call-done = (bf16[2,128,64]{1,2,0:T(8,128)(2,1)}, bf16[2,128,64]{1,2,0:T(8,128)(2,1)}) async-done(((bf16[2,128,64]{1,2,0:T(8,128)(2,1)}, bf16[2,128,64]{1,2,0:T(8,128)(2,1)}), (bf16[2,128,64]{1,2,0:T(8,128)(2,1)}, bf16[2,128,64]{1,2,0:T(8,128)(2,1)})) %all-reduce.3.cloned.1.call-update) | async-done | bytes 65552 | tf_op jit(solution)/shard_map/psum | solution.py:64
  296.4 0.9 fusion.25
  297.3 0.7 convolution_convert_fusion.2
  298.0 1.7 copy.58
  299.8 0.0 copy-start.2
  299.8 0.0 reduce-scatter.6.cloned.1.call-update
  299.8 0.0 reduce-scatter.8.cloned.1.call-start
  299.8 0.7 copy-done.2
  300.5 0.2 convolution_multiply_fusion.1
  300.7 0.7 convolution_convert_fusion.1
  301.4 1.7 copy.61
  303.1 0.0 reduce-scatter.8.cloned.1.call-update
  303.2 0.0 reduce-scatter.4.cloned.1.call-start
  303.2 5.4 convolution_convert_fusion
  308.6 0.0 copy-start.3
  308.6 0.0 reduce-scatter.4.cloned.1.call-update
  308.6 0.7 copy-done.3
  309.4 0.2 fusion.22
  309.6 0.1 copy.66
  309.7 0.2 convolution_multiply_fusion
  310.0 5.4 fusion.4
  315.4 72.4 %reduce-scatter.6.cloned.1.call-done = bf16[2,64,256]{2,1,0:T(8,128)(2,1)} async-done(((bf16[48,64,256]{2,1,0:T(8,128)(2,1)}), bf16[2,64,256]{2,1,0:T(8,128)(2,1)}) %reduce-scatter.6.cloned.1.call-update) | async-done | bytes 65552 | tf_op jit(solution)/shard_map/reduce_scatter | solution.py:99
  387.8 1.2 convolution_convert_fusion.4
  389.0 1.0 copy.64
  390.0 85.9 %reduce-scatter.8.cloned.1.call-done = bf16[2,64,256]{2,1,0:T(8,128)(2,1)} async-done(((bf16[48,64,256]{2,1,0:T(8,128)(2,1)}), bf16[2,64,256]{2,1,0:T(8,128)(2,1)}) %reduce-scatter.8.cloned.1.call-update) | async-done | bytes 65552 | tf_op jit(solution)/shard_map/reduce_scatter | solution.py:100
  475.9 1.2 convolution_convert_fusion.3
  477.1 1.0 copy.65
  478.1 230.7 %reduce-scatter.4.cloned.1.call-done = bf16[256,256]{1,0:T(8,128)(2,1)} async-done(((bf16[8192,256]{1,0:T(8,128)(2,1)}), bf16[256,256]{1,0:T(8,128)(2,1)}) %reduce-scatter.4.cloned.1.call-update) | async-done | bytes 131088 | tf_op jit(solution)/shard_map/reduce_scatter | solution.py:74
  708.8 0.9 fusion.14
  709.7 0.8 copy.63
  (6 shorter events, 0.1 us)
Async XLA Ops:
  7.2 1.2 copy-start
  7.2 4.5 copy-start.4
  7.2 71.7 %all-gather.3.cloned.1.call-start = ((), (), s32[]{:S(2)}) async-start(), calls=%async_computation.3 | async-start | bytes 1638400 | tf_op jit(solution)/shard_map/all_gather | solution.py:52
  9.4 129.3 %all-gather.5.cloned.1.call-start = ((), (), s32[]{:S(2)}) async-start(), calls=%async_computation.4 | async-start | bytes 1638400 | tf_op jit(solution)/shard_map/all_gather | solution.py:53
  11.6 284.8 %all-reduce.3.cloned.1.call-start = ((), (), s32[]{:S(2)}) async-start(), calls=%async_computation.8 | async-start | bytes 131072 | tf_op jit(solution)/shard_map/psum | solution.py:64
  13.4 127.6 %copy-start.1 = (bf16[256,256]{1,0:T(8,128)(2,1)S(1)}, bf16[256,256]{1,0:T(8,128)(2,1)}, u32[]{:S(2)}) copy-start(bf16[256,256]{1,0:T(8,128)(2,1)} %param.10) | copy-start | bytes 393220
  141.9 245.9 %reduce-scatter.6.cloned.1.call-start = ((), (), s32[]{:S(2)}) async-start(), calls=%async_computation.6 | async-start | bytes 1638400 | tf_op jit(solution)/shard_map/reduce_scatter | solution.py:99
  299.8 0.8 copy-start.2
  299.8 176.1 %reduce-scatter.8.cloned.1.call-start = ((), (), s32[]{:S(2)}) async-start(), calls=%async_computation.7 | async-start | bytes 1638400 | tf_op jit(solution)/shard_map/reduce_scatter | solution.py:100
  303.2 405.6 %reduce-scatter.4.cloned.1.call-start = ((), (), s32[]{:S(2)}) async-start(), calls=%async_computation.5 | async-start | bytes 4325376 | tf_op jit(solution)/shard_map/reduce_scatter | solution.py:74
  308.6 0.8 copy-start.3
Sparse Core Ops, SparseCore 0:
  11.0 67.8 all-gather.2
  81.9 56.7 all-gather.4
  142.8 153.5 all-reduce.2
  299.9 87.8 reduce-scatter.5
  391.0 84.7 reduce-scatter.7
  480.8 227.9 reduce-scatter.3
where the time goes:
time: 721 us; the launch traced here: 717 us
  waiting for transfers between devices  666 us (92%)
  matrix products  24.3 us (3%)
  between operations  14.2 us (2%)
  local copies, waits for them, and re-layouts  10.7 us (1%)
    reduce_scatter x1, waiting for transfers between devices, per_device(): lax.psum_scatter(lax.dot_general(projection_weight, output_gradient, (((1...  231 us
    psum x1, waiting for transfers between devices, per_device(): low_rank = lax.psum(down_part.astype(jnp.bfloat16), 'tensor')  154 us
    reduce_scatter x1, waiting for transfers between devices, per_device(): lax.psum_scatter(slot_up, 'adapter', scatter_dimension=0, tiled=True)  85.9 us
    reduce_scatter x1, waiting for transfers between devices, per_device(): lax.psum_scatter(slot_down, 'adapter', scatter_dimension=0, tiled=True)  72.4 us
    all_gather x1, waiting for transfers between devices, per_device(): lax.all_gather(packed_down, 'adapter', axis=0, tiled=True)  65.5 us
    all_gather x1, waiting for transfers between devices, per_device(): lax.all_gather(packed_up, 'adapter', axis=0, tiled=True)  56.6 us
  transfers between devices with their start and end apart: 6, of which 6 were waited for; matrix products, arithmetic and copies ran while one was open for 4% of the time, Pallas kernels for 0%

commit v1 on v0

v1 whole, which is shorter than its diff:
```python
import functools

import jax
import jax.numpy as jnp
from jax import lax
from jax.experimental import pallas as pl
from jax.experimental.pallas import tpu as pltpu
from jax.sharding import PartitionSpec as P

SEG_ROWS = 128
ADP_OWN = 16
ACTIVE = 2
RANK = 64
COLS = 256
X_CHIPS = 4
MESH = pl.DeviceIdType.MESH
F32 = jnp.float32
BF16 = jnp.bfloat16

adapter_scale = 0.5


def dot(a, b, ca, cb):
    return lax.dot_general(a, b, (((ca,), (cb,)), ((), ())), preferred_element_type=F32)


def chains_of(n):
    half = n // 2
    chains, base = [], 0
    for sign, part, length in ((1, 0, half), (-1, 1, half), (1, 1, half - 1), (-1, 0, half - 1)):
        if length:
            chains.append((sign, part, length, base))
            base += length
    return chains, base


class RingSum:
    def __init__(self, n, pos, device_of, src, land, send_sem, recv_sem):
        self.n, self.pos, self.device_of = n, pos, device_of
        self.src, self.land, self.send_sem, self.recv_sem = src, land, send_sem, recv_sem
        self.chains, _ = chains_of(n)
        self.steps = n // 2

    def at(self, offset):
        return lax.rem(self.pos + offset + self.n, self.n)

    def copy(self, src, slot, sign):
        return pltpu.make_async_remote_copy(
            src_ref=src,
            dst_ref=self.land.at[slot],
            send_sem=self.send_sem,
            recv_sem=self.recv_sem.at[slot],
            device_id={"tensor": self.device_of(self.at(sign))},
            device_id_type=MESH,
        )

    def start(self):
        for sign, part, length, base in self.chains:
            self.copy(self.src.at[self.at(sign * length), part], base, sign).start()

    def step(self, s):
        for sign, part, length, base in self.chains:
            if s >= length - 1:
                continue
            slot = base + s
            self.copy(self.land.at[slot], slot, sign).wait_recv()
            place = self.at(sign * (length - s - 1))
            self.add(slot, place, part)
            self.copy(self.land.at[slot], slot + 1, sign).start()

    def add(self, slot, place, part):
        if len(self.land.shape) == 3:
            total = self.land[slot].astype(F32) + self.src[place, part].astype(F32)
            self.land[slot] = total.astype(BF16)
            return

        def body(j, carry):
            total = self.land[slot, j].astype(F32) + self.src[place, part, j].astype(F32)
            self.land[slot, j] = total.astype(BF16)
            return carry

        lax.fori_loop(0, self.land.shape[1], body, 0)

    def finish(self):
        for sign, part, length, base in self.chains:
            slot = base + length - 1
            self.copy(self.land.at[slot], slot, sign).wait_recv()

    def lasts(self, part):
        return [base + length - 1 for _, p, length, base in self.chains if p == part]

    def total(self, part, *index):
        value = self.src[(self.pos, part) + index].astype(F32)
        for slot in self.lasts(part):
            value = value + self.land[(slot,) + index].astype(F32)
        return value

    def drain(self):
        whole = self.src.at[pl.ds(0, self.n - 1)]
        pltpu.make_async_remote_copy(
            src_ref=whole,
            dst_ref=whole,
            send_sem=self.send_sem,
            recv_sem=self.recv_sem.at[0],
            device_id={"tensor": self.device_of(self.at(1))},
            device_id_type=MESH,
        ).wait_send()


class RingGather:
    def __init__(self, n, z, core, own, out, send_sem, recv_sem, pair_sem, own_sem):
        self.n, self.z, self.core = n, z, core
        self.own, self.out = own, out
        self.send_sem, self.recv_sem, self.pair_sem, self.own_sem = send_sem, recv_sem, pair_sem, own_sem
        self.steps = n // 2

    def has(self, d, k, ch):
        return k < self.steps - 1 or (k == self.steps - 1 and d == ch)

    def rows(self, z, core, ch):
        return self.out.at[pl.ds((z * 2 + core) * 4 + ch * 2, 2)]

    def ring(self, src, dst, d, k, ch):
        sign = 1 - 2 * d
        z_to = lax.rem(self.z + sign + self.n, self.n)
        return pltpu.make_async_remote_copy(
            src_ref=src,
            dst_ref=dst,
            send_sem=self.send_sem,
            recv_sem=self.recv_sem.at[d, k, ch],
            device_id={"adapter": z_to * 2 + self.core},
            device_id_type=MESH,
        )

    def pair(self, src, dst):
        return pltpu.make_async_remote_copy(
            src_ref=src,
            dst_ref=dst,
            send_sem=self.send_sem,
            recv_sem=self.pair_sem,
            device_id={"adapter": self.z * 2 + 1 - self.core},
            device_id_type=MESH,
        )

    def own_copy(self):
        return pltpu.make_async_copy(
            self.own, self.out.at[pl.ds((self.z * 2 + self.core) * 4, 4)], self.own_sem
        )

    def start(self):
        for ch in range(2):
            src, dst = self.own.at[pl.ds(ch * 2, 2)], self.rows(self.z, self.core, ch)
            for d in range(2):
                if self.has(d, 0, ch):
                    self.ring(src, dst, d, 0, ch).start()
        for ch in range(2):
            src, dst = self.own.at[pl.ds(ch * 2, 2)], self.rows(self.z, self.core, ch)
            self.pair(src, dst).start()
        self.own_copy().start()

    def step(self, k):
        for ch in range(2):
            for d in range(2):
                if not self.has(d, k, ch):
                    continue
                sign = 1 - 2 * d
                z_from = lax.rem(self.z - sign * (k + 1) + 2 * self.n, self.n)
                block = self.rows(z_from, self.core, ch)
                self.ring(block, block, d, k, ch).wait_recv()
                if self.has(d, k + 1, ch):
                    self.ring(block, block, d, k + 1, ch).start()
                self.pair(block, block).start()

    def finish(self):
        self.own_copy().wait()
        half = self.out.at[pl.ds(0, self.n * 4)]
        self.pair(half, half).wait_recv()

    def drain(self):
        sent = self.out.at[pl.ds(0, (4 * self.n - 2) * 2)]
        self.pair(sent, sent).wait_send()


def step_kernel(
    owners, tensors,
    idx, mask, x_hbm, w_hbm, down_ref, up_ref, g_ref,
    po_ref, gi_ref, dg_ref, ug_ref,
    xv, wv, acc, pk, ga, gk, gb, f1, f2, r1, r2, s1, s2, q1, q2, part, inbox, mine, total,
    in_sem, own_sem, gs_a, gr_a, gp_a, gs_b, gr_b, gp_b,
    s_r1, v_r1, s_r2, v_r2, s_q1, v_q1, s_q2, v_q2, ar_send, ar_recv,
):
    nz, nx = owners // 2, X_CHIPS
    ny = tensors // nx
    hx, hy = nx // 2, ny // 2
    me_a, me_t = lax.axis_index("adapter"), lax.axis_index("tensor")
    z, core = lax.div(me_a, 2), lax.rem(me_a, 2)
    y, x = lax.div(me_t, nx), lax.rem(me_t, nx)

    barrier = pltpu.get_barrier_semaphore()
    for to in (lax.rem(z + 1, nz) * 2 + core, lax.rem(z + nz - 1, nz) * 2 + core, z * 2 + 1 - core):
        pl.semaphore_signal(barrier, inc=1, device_id={"adapter": to}, device_id_type=MESH)

    def greet(d, carry):
        to = lax.rem(me_t + d, tensors)
        pl.semaphore_signal(barrier, inc=1, device_id={"tensor": to}, device_id_type=MESH)
        return carry

    lax.fori_loop(1, tensors, greet, 0)
    w_in = pltpu.make_async_copy(w_hbm, wv, in_sem.at[0])
    x_in = pltpu.make_async_copy(x_hbm, xv, in_sem.at[1])
    w_in.start()
    x_in.start()
    for j in range(ACTIVE):
        pk[j] = down_ref[idx[j]]
        pk[ACTIVE + j] = up_ref[idx[j]]
    pl.semaphore_wait(barrier, tensors + 2)

    panels = RingGather(nz, z, core, pk, ga, gs_a, gr_a, gp_a, own_sem.at[0])
    parts = RingGather(nz, z, core, gk, gb, gs_b, gr_b, gp_b, own_sem.at[1])
    along_x = lambda place: y * nx + place
    along_y = lambda place: place * nx + x
    sum_x1 = RingSum(nx, x, along_x, f1, r1, s_r1, v_r1)
    sum_y1 = RingSum(ny, y, along_y, f2, r2, s_r2, v_r2)
    sum_y2 = RingSum(ny, y, along_y, s1, q1, s_q1, v_q1)
    sum_x2 = RingSum(nx, x, along_x, s2, q2, s_q2, v_q2)

    panels.start()
    w_in.wait()

    def frozen_term(t, carry):
        term = dot(g_ref[...], wv[t], 1, 1).astype(BF16)
        ty, tx = lax.div(t, nx), lax.rem(t, nx)
        f1[tx, lax.div(ty, hy), lax.rem(ty, hy)] = term[:SEG_ROWS]
        f2[ty, lax.div(tx, hx), lax.rem(tx, hx)] = term[SEG_ROWS:]
        return carry

    lax.fori_loop(0, tensors, frozen_term, 0)
    sum_x1.start()
    sum_y1.start()
    panels.step(0)
    order = []
    for k in range(1, max(panels.steps, sum_y1.steps)):
        order += [(sum_y1, k - 1), (sum_x1, k - 1), (panels, k)]
    for ring, k in order:
        if k < ring.steps:
            ring.step(k)
    panels.finish()

    x_in.wait()
    col0 = pl.multiple_of(me_t * COLS, COLS)
    for s in range(2):
        rows = slice(s * SEG_ROWS, (s + 1) * SEG_ROWS)
        low = dot(xv[rows, pl.ds(col0, COLS)], ga[idx[2 + s]], 1, 1)
        back = dot(g_ref[rows, :], ga[idx[2 + s] + ACTIVE], 1, 1)
        both = jnp.concatenate([low, back], axis=1)
        per = tensors // 2
        part[s * per:(s + 1) * per] = both.reshape(per, SEG_ROWS // per, 2 * RANK)

    def to_peer(src, dst, phase, d):
        return pltpu.make_async_remote_copy(
            src_ref=src, dst_ref=dst, send_sem=ar_send.at[phase], recv_sem=ar_recv.at[phase],
            device_id={"tensor": lax.rem(me_t + d, tensors)}, device_id_type=MESH,
        )

    def scatter(d, carry):
        to_peer(part.at[lax.rem(me_t + d, tensors)], inbox.at[d - 1], 0, d).start()
        return carry

    lax.fori_loop(1, tensors, scatter, 0)

    acc[...] = jnp.zeros_like(acc)

    def forward(k, carry):
        at = pl.multiple_of(k * COLS, COLS)
        acc[...] += dot(xv[:, pl.ds(at, COLS)], wv[k], 1, 0)
        return carry

    lax.fori_loop(0, tensors, forward, 0)

    others = inbox.at[pl.ds(0, tensors - 1)]
    to_peer(others, others, 0, 1).wait_recv()
    value = part[me_t]
    for d in range(tensors - 1):
        value = value + inbox[d]
    mine[...] = value
    total[me_t] = value

    def spread(d, carry):
        to_peer(mine, total.at[me_t], 1, d).start()
        return carry

    lax.fori_loop(1, tensors, spread, 0)

    sum_x1.finish()
    sum_y1.finish()
    for h in range(2):
        def first_x(j, carry):
            v = sum_x1.total(h, j).astype(BF16)
            s1[h * hy + j, 0] = v[:RANK]
            s1[h * hy + j, 1] = v[RANK:]
            return carry

        def first_y(j, carry):
            v = sum_y1.total(h, j).astype(BF16)
            s2[h * hx + j, 0] = v[:RANK]
            s2[h * hx + j, 1] = v[RANK:]
            return carry

        lax.fori_loop(0, hy, first_x, 0)
        lax.fori_loop(0, hx, first_y, 0)
    rest = total.at[pl.ds(0, tensors - 1)]
    to_peer(rest, rest, 1, 1).wait_recv()

    ranks = total[...].reshape(2 * SEG_ROWS, 2 * RANK)
    halves, downs, ups = [], [], []
    for s in range(2):
        rows = slice(s * SEG_ROWS, (s + 1) * SEG_ROWS)
        low_half = ranks[rows, :RANK].astype(BF16)
        back_half = (adapter_scale * ranks[rows, RANK:]).astype(BF16)
        halves.append((low_half, back_half))
        downs.append(dot(back_half, xv[rows, pl.ds(col0, COLS)], 0, 0))
        ups.append(adapter_scale * dot(low_half, g_ref[rows, :], 0, 0))
    same = mask[0]
    for base, terms in ((0, downs), (ACTIVE, ups)):
        gk[base] = (terms[0] + same * terms[1]).astype(BF16)
        gk[base + 1] = ((1.0 - same) * terms[1]).astype(BF16)
    parts.start()
    sum_y2.start()
    sum_x2.start()
    for s in range(2):
        rows = slice(s * SEG_ROWS, (s + 1) * SEG_ROWS)
        low_half, back_half = halves[s]
        adapted = dot(low_half, ga[idx[2 + s] + ACTIVE], 1, 0)
        po_ref[rows, :] = (acc[rows, :] + adapter_scale * adapted).astype(BF16)
        acc[rows, :] = dot(back_half, ga[idx[2 + s]], 1, 0)
    for k in range(max(parts.steps, sum_y2.steps)):
        for ring in (parts, sum_y2, sum_x2):
            if k < ring.steps:
                ring.step(k)
        if k == sum_y2.steps - 1:
            sum_y2.finish()
            sum_x2.finish()
            for s, ring in ((0, sum_y2), (1, sum_x2)):
                for h in range(2):
                    rows = slice(s * SEG_ROWS + h * RANK, s * SEG_ROWS + (h + 1) * RANK)
                    gi_ref[rows, :] = (ring.total(h) + acc[rows, :]).astype(BF16)
    parts.finish()

    segs = owners * ACTIVE
    for base, out in ((0, dg_ref), (ACTIVE, ug_ref)):
        def gather(i, carry):
            g, s = lax.div(i, 2), lax.rem(i, 2)
            block = gb[g * 4 + base + s].astype(F32)
            return carry[0] + mask[1 + i] * block, carry[1] + mask[1 + segs + i] * block

        zero = jnp.zeros((RANK, COLS), F32)
        first, second = lax.fori_loop(0, segs, gather, (zero, zero))

        def place(i, carry):
            at = 1 + 2 * segs + i
            out[i] = (mask[at] * first + mask[at + ADP_OWN] * second).astype(BF16)
            return carry

        lax.fori_loop(0, ADP_OWN, place, 0)

    panels.drain()
    parts.drain()
    for ring in (sum_x1, sum_y1, sum_y2, sum_x2):
        ring.drain()
    to_peer(others, others, 0, 1).wait_send()
    to_peer(others, others, 1, 1).wait_send()


def per_device(
    rollout_activations,
    projection_weight,
    adapter_down_panels,
    adapter_up_panels,
    output_gradient,
    segment_adapter,
):
    owners, tensors = lax.axis_size("adapter"), lax.axis_size("tensor")
    nz, nx = owners // 2, X_CHIPS
    ny = tensors // nx
    me = lax.axis_index("adapter")
    all_ids = jnp.arange(owners * ADP_OWN, dtype=jnp.int32)
    use = jnp.any(segment_adapter[:, None] == all_ids[None, :], axis=0)
    grid = use.reshape(owners, ADP_OWN).astype(jnp.int32)
    rank = jnp.cumsum(grid, axis=1) - 1
    group_ids = lax.dynamic_slice_in_dim(segment_adapter, me * 2, 2)
    slot = jnp.sum(
        jnp.where(group_ids[:, None] == all_ids[None, :], rank.reshape(1, -1), 0), axis=1
    )
    own_use = lax.dynamic_index_in_dim(grid, me, 0, keepdims=False)
    own_rank = lax.dynamic_index_in_dim(rank, me, 0, keepdims=False)
    picker = (own_rank[None, :] == jnp.arange(ACTIVE, dtype=jnp.int32)[:, None]) & (
        own_use[None, :] > 0
    )
    own_local = jnp.sum(jnp.where(picker, jnp.arange(ADP_OWN, dtype=jnp.int32)[None, :], 0), axis=1)
    idx = jnp.concatenate([own_local, (group_ids // ADP_OWN) * 4 + slot]).astype(jnp.int32)
    own_named = jnp.any(picker, axis=1)
    named = own_named[:, None] & (segment_adapter[None, :] == (me * ADP_OWN + own_local)[:, None])
    same = (group_ids[0] == group_ids[1]).reshape(1)
    mask = jnp.concatenate([same, named.reshape(-1), picker.reshape(-1)]).astype(F32)

    rows, width = rollout_activations.shape
    blocks = owners * 4
    slots_x, slots_y = chains_of(nx)[1], chains_of(ny)[1]
    vmem = pltpu.VMEM
    dma, block = pltpu.SemaphoreType.DMA, (RANK, COLS)
    gather_sems = [dma(()), dma((2, nz // 2, 2)), dma(())]
    seg = (SEG_ROWS, COLS)
    scratch = [
        vmem((rows, width), BF16),
        vmem((tensors, COLS, COLS), BF16),
        vmem((rows, COLS), F32),
        vmem((4,) + block, BF16),
        vmem((blocks,) + block, BF16),
        vmem((4,) + block, BF16),
        vmem((blocks,) + block, BF16),
        vmem((nx, 2, ny // 2) + seg, BF16),
        vmem((ny, 2, nx // 2) + seg, BF16),
        vmem((slots_x, ny // 2) + seg, BF16),
        vmem((slots_y, nx // 2) + seg, BF16),
        vmem((ny, 2) + block, BF16),
        vmem((nx, 2) + block, BF16),
        vmem((slots_y,) + block, BF16),
        vmem((slots_x,) + block, BF16),
        vmem((tensors, rows // tensors, 2 * RANK), F32),
        vmem((tensors, rows // tensors, 2 * RANK), F32),
        vmem((rows // tensors, 2 * RANK), F32),
        vmem((tensors, rows // tensors, 2 * RANK), F32),
        dma((2,)),
        dma((2,)),
        *gather_sems,
        *gather_sems,
    ]
    for slots in (slots_x, slots_y, slots_y, slots_x):
        scratch += [dma(()), dma((slots,))]
    scratch += [dma((2,)), dma((2,))]
    smem, whole, any_space = (
        pl.BlockSpec(memory_space=pltpu.SMEM),
        pl.BlockSpec(memory_space=pltpu.VMEM),
        pl.BlockSpec(memory_space=pl.ANY),
    )
    out = [
        jax.ShapeDtypeStruct((rows, COLS), BF16),
        jax.ShapeDtypeStruct((rows, COLS), BF16),
        jax.ShapeDtypeStruct((ADP_OWN,) + block, BF16),
        jax.ShapeDtypeStruct((ADP_OWN,) + block, BF16),
    ]
    return tuple(
        pl.pallas_call(
            functools.partial(step_kernel, owners, tensors),
            out_shape=out,
            in_specs=[smem, smem, any_space, any_space, whole, whole, whole],
            out_specs=[whole] * 4,
            scratch_shapes=scratch,
            compiler_params=pltpu.CompilerParams(
                collective_id=0, has_side_effects=True, vmem_limit_bytes=60 * 1024 * 1024
            ),
        )(
            idx,
            mask,
            rollout_activations,
            projection_weight.reshape(tensors, COLS, COLS),
            adapter_down_panels,
            adapter_up_panels,
            output_gradient,
        )
    )


def solution(mesh):
    in_specs = (
        P("adapter", None),
        P(None, "tensor"),
        P("adapter", None, "tensor"),
        P("adapter", None, "tensor"),
        P("adapter", "tensor"),
        P(),
    )
    out_specs = (
        P("adapter", "tensor"),
        P("adapter", "tensor"),
        P("adapter", None, "tensor"),
        P("adapter", None, "tensor"),
    )
    return jax.shard_map(
        per_device, mesh=mesh, in_specs=in_specs, out_specs=out_specs, check_vma=False
    )
```

time: 721 us -> 116 us (0.16)
  waiting for transfers between devices: 666 us -> 0 us
  Pallas kernels: 0 us -> 101 us
  matrix products: 24.3 us -> 0 us
  between operations: 14.2 us -> 1.97 us
    reduce_scatter x3 -> x0, waiting for transfers between devices: 389 us -> none  [the longest x1 231 us: per_device(): lax.psum_scatter(lax.dot_general(projection_weight, output_gradient, (((1...]
    psum x1 -> x0, waiting for transfers between devices: 154 us -> none  [per_device(): low_rank = lax.psum(down_part.astype(jnp.bfloat16), 'tensor')]
    all_gather x2 -> x0, waiting for transfers between devices: 122 us -> none  [the longest x1 65.5 us: per_device(): lax.all_gather(packed_down, 'adapter', axis=0, tiled=True)]
    pallas_call x0 -> x1, Pallas kernels: none -> 101 us  [per_device(): pl.pallas_call(functools.partial(step_kernel, owners, tensors), out_shape...]
    dot_general x16 -> x0, matrix products: 24.3 us -> none  [the longest x1 5.41 us: per_device(): lax.dot_general(projection_weight, output_gradient, (((1,), (1,)), ((), (...]
  transfers between devices with their start and end apart: 6 -> 0, of which waited for: 6 -> 0; matrix products, arithmetic and copies ran while one was open for 4% -> 0% of each run, Pallas kernels for 0% -> 0%
where the time goes in v1:
time: 116 us; the launch traced here: 115 us
  Pallas kernels  101 us (87%)
  local copies, waits for them, and re-layouts  8.55 us (7%)
  other arithmetic  4.06 us (3%)
  between operations  1.97 us (2%)
    pallas_call x1, Pallas kernels, per_device(): pl.pallas_call(functools.partial(step_kernel, owners, tensors), out_shape...  101 us
    unnamed x4, local copies, waits for them, and re-layouts  6.9 us

profile of v1, /device:TPU:1, one launch (start us, length us, event | category | flops | bytes accessed | tf_op | source)
XLA Modules:
  0.0 115.2 jit_solution(4451419115577263092)
XLA Ops:
  0.6 0.7 dynamic_slice.12
  1.4 0.7 fusion
  2.1 0.6 fusion.3
  4.0 0.1 reshape.45
  4.1 0.2 reduce_window_sum.11
  4.3 0.1 sub.12
  4.4 0.2 fusion.1
  4.6 0.7 multiply_add_fusion
  5.3 0.1 fusion.2
  5.4 0.1 select_reduce_fusion
  5.5 0.1 and.38
  5.6 0.6 pad_add_fusion.idx
  6.2 0.7 compare_and_fusion
  6.9 0.1 and.37
  7.0 0.6 add_convert_fusion.mask
  7.7 100.6 %shard_map.93 = (bf16[256,256]{1,0:T(8,128)(2,1)}, bf16[256,256]{1,0:T(8,128)(2,1)}, bf16[16,64,256]{2,1,0:T(8,128)(2,1)}, bf16[16,64,256]{2,1,0:T(8,128)(2,1)}) custom-call(s32[4]{0:T(128)} %pad_add_fusion.idx, f32[129]{0:T(256)} %add_convert_fusion.mask, bf16[256,8192]{1,0:T(8,128)(2,1)} %x_hbm.1, bf16[32,256,256]{2,1,0:T(8,128)(2,1)} %bitcast.5, ...), custom_call_target="tpu_custom_call" | custom-call | tf_op jit(solution)/shard_map/pallas_call | solution.py:453
  108.3 1.6 %copy.14 = bf16[256,256]{1,0:T(8,128)(2,1)} copy(bf16[256,256]{1,0:T(8,128)(2,1)} %get-tuple-element.12) | data formatting | bytes 262144
  109.9 1.6 %copy.15 = bf16[256,256]{1,0:T(8,128)(2,1)} copy(bf16[256,256]{1,0:T(8,128)(2,1)} %get-tuple-element.13) | data formatting | bytes 262144
  111.4 1.9 %copy.16 = bf16[16,64,256]{2,1,0:T(8,128)(2,1)} copy(bf16[16,64,256]{2,1,0:T(8,128)(2,1)} %get-tuple-element.14) | data formatting | bytes 1048576
  113.3 1.9 %copy.17 = bf16[16,64,256]{2,1,0:T(8,128)(2,1)} copy(bf16[16,64,256]{2,1,0:T(8,128)(2,1)} %get-tuple-element.15) | data formatting | bytes 1048576
  (5 shorter events, 0.0 us)

commit v2 on v1

--- a/solution.py
+++ b/solution.py
@@ -132,12 +132,12 @@
             device_id_type=MESH,
         )
 
-    def pair(self, src, dst):
+    def pair(self, src, dst, k):
         return pltpu.make_async_remote_copy(
             src_ref=src,
             dst_ref=dst,
             send_sem=self.send_sem,
-            recv_sem=self.pair_sem,
+            recv_sem=self.pair_sem.at[k],
             device_id={"adapter": self.z * 2 + 1 - self.core},
             device_id_type=MESH,
         )
@@ -155,7 +155,7 @@
                     self.ring(src, dst, d, 0, ch).start()
         for ch in range(2):
             src, dst = self.own.at[pl.ds(ch * 2, 2)], self.rows(self.z, self.core, ch)
-            self.pair(src, dst).start()
+            self.pair(src, dst, 0).start()
         self.own_copy().start()
 
     def step(self, k):
@@ -169,23 +169,43 @@
                 self.ring(block, block, d, k, ch).wait_recv()
                 if self.has(d, k + 1, ch):
                     self.ring(block, block, d, k + 1, ch).start()
-                self.pair(block, block).start()
-
-    def finish(self):
-        self.own_copy().wait()
-        half = self.out.at[pl.ds(0, self.n * 4)]
-        self.pair(half, half).wait_recv()
+                self.pair(block, block, k + 1).start()
+
+    def pair_wait(self, k):
+        count = 2 if k == 0 else sum(self.has(d, k - 1, ch) for d in range(2) for ch in range(2))
+        landed = self.out.at[pl.ds(0, 2 * count)]
+        self.pair(landed, landed, k).wait_recv()
+
+    def places(self, k):
+        return [self.z] if k == 0 else [
+            lax.rem(self.z + sign * k + self.n, self.n) for sign in ((1, -1) if k < self.steps else (1,))
+        ]
 
     def drain(self):
         sent = self.out.at[pl.ds(0, (4 * self.n - 2) * 2)]
-        self.pair(sent, sent).wait_send()
+        self.pair(sent, sent, 0).wait_send()
+
+
+def named_range(ids, segs, owner):
+    start = owner * ADP_OWN
+
+    def body(i, carry):
+        low, high = carry
+        v = ids[i]
+        held = (v >= start) & (v < start + ADP_OWN)
+        return (
+            jnp.where(held, jnp.minimum(low, v), low),
+            jnp.where(held, jnp.maximum(high, v), high),
+        )
+
+    return lax.fori_loop(0, segs, body, (start + ADP_OWN, start - 1))
 
 
 def step_kernel(
     owners, tensors,
-    idx, mask, x_hbm, w_hbm, down_ref, up_ref, g_ref,
-    po_ref, gi_ref, dg_ref, ug_ref,
-    xv, wv, acc, pk, ga, gk, gb, f1, f2, r1, r2, s1, s2, q1, q2, part, inbox, mine, total,
+    ids, x_hbm, w_hbm, down_ref, up_ref, g_ref,
+    po_ref, gi_ref, sums_ref,
+    asum, xv, wv, acc, pk, ga, gk, gb, f1, f2, r1, r2, s1, s2, q1, q2, part, inbox, mine, total,
     in_sem, own_sem, gs_a, gr_a, gp_a, gs_b, gr_b, gp_b,
     s_r1, v_r1, s_r2, v_r2, s_q1, v_q1, s_q2, v_q2, ar_send, ar_recv,
 ):
@@ -210,10 +230,12 @@
     x_in = pltpu.make_async_copy(x_hbm, xv, in_sem.at[1])
     w_in.start()
     x_in.start()
-    for j in range(ACTIVE):
-        pk[j] = down_ref[idx[j]]
-        pk[ACTIVE + j] = up_ref[idx[j]]
-    pl.semaphore_wait(barrier, tensors + 2)
+    segs = owners * 2
+    own_low, own_high = named_range(ids, segs, me_a)
+    for j, v in enumerate((own_low, own_high)):
+        local = jnp.clip(v - me_a * ADP_OWN, 0, ADP_OWN - 1)
+        pk[j] = down_ref[local]
+        pk[ACTIVE + j] = up_ref[local]
 
     panels = RingGather(nz, z, core, pk, ga, gs_a, gr_a, gp_a, own_sem.at[0])
     parts = RingGather(nz, z, core, gk, gb, gs_b, gr_b, gp_b, own_sem.at[1])
@@ -224,7 +246,6 @@
     sum_y2 = RingSum(ny, y, along_y, s1, q1, s_q1, v_q1)
     sum_x2 = RingSum(nx, x, along_x, s2, q2, s_q2, v_q2)
 
-    panels.start()
     w_in.wait()
 
     def frozen_term(t, carry):
@@ -235,23 +256,33 @@
         return carry
 
     lax.fori_loop(0, tensors, frozen_term, 0)
+    pl.semaphore_wait(barrier, tensors + 2)
+    panels.start()
     sum_x1.start()
     sum_y1.start()
-    panels.step(0)
-    order = []
-    for k in range(1, max(panels.steps, sum_y1.steps)):
-        order += [(sum_y1, k - 1), (sum_x1, k - 1), (panels, k)]
+    seg_block = []
+    for s in range(2):
+        v = ids[me_a * 2 + s]
+        owner = lax.div(v, ADP_OWN)
+        low, _ = named_range(ids, segs, owner)
+        seg_block.append(owner * 4 + jnp.where(v > low, 1, 0))
+    same = jnp.where(ids[me_a * 2] == ids[me_a * 2 + 1], 1.0, 0.0).astype(F32)
+    asum[...] = jnp.zeros_like(asum)
+    order = [(panels, 0), (panels, 1), (sum_y1, 0), (sum_x1, 0), (panels, 2), (panels, 3), (panels, 4), (sum_y1, 1)]
+    order += [(panels, k) for k in range(5, panels.steps)]
     for ring, k in order:
         if k < ring.steps:
             ring.step(k)
-    panels.finish()
+    panels.own_copy().wait()
+    for k in range(panels.steps + 1):
+        panels.pair_wait(k)
 
     x_in.wait()
     col0 = pl.multiple_of(me_t * COLS, COLS)
     for s in range(2):
         rows = slice(s * SEG_ROWS, (s + 1) * SEG_ROWS)
-        low = dot(xv[rows, pl.ds(col0, COLS)], ga[idx[2 + s]], 1, 1)
-        back = dot(g_ref[rows, :], ga[idx[2 + s] + ACTIVE], 1, 1)
+        low = dot(xv[rows, pl.ds(col0, COLS)], ga[seg_block[s]], 1, 1)
+        back = dot(g_ref[rows, :], ga[seg_block[s] + ACTIVE], 1, 1)
         both = jnp.concatenate([low, back], axis=1)
         per = tensors // 2
         part[s * per:(s + 1) * per] = both.reshape(per, SEG_ROWS // per, 2 * RANK)
@@ -291,8 +322,9 @@
 
     lax.fori_loop(1, tensors, spread, 0)
 
+    for k in range(2, sum_y1.steps):
+        sum_y1.step(k)
     sum_x1.finish()
-    sum_y1.finish()
     for h in range(2):
         def first_x(j, carry):
             v = sum_x1.total(h, j).astype(BF16)
@@ -300,14 +332,7 @@
             s1[h * hy + j, 1] = v[RANK:]
             return carry
 
-        def first_y(j, carry):
-            v = sum_y1.total(h, j).astype(BF16)
-            s2[h * hx + j, 0] = v[:RANK]
-            s2[h * hx + j, 1] = v[RANK:]
-            return carry
-
         lax.fori_loop(0, hy, first_x, 0)
-        lax.fori_loop(0, hx, first_y, 0)
     rest = total.at[pl.ds(0, tensors - 1)]
     to_peer(rest, rest, 1, 1).wait_recv()
 
@@ -320,48 +345,74 @@
         halves.append((low_half, back_half))
         downs.append(dot(back_half, xv[rows, pl.ds(col0, COLS)], 0, 0))
         ups.append(adapter_scale * dot(low_half, g_ref[rows, :], 0, 0))
-    same = mask[0]
     for base, terms in ((0, downs), (ACTIVE, ups)):
         gk[base] = (terms[0] + same * terms[1]).astype(BF16)
         gk[base + 1] = ((1.0 - same) * terms[1]).astype(BF16)
     parts.start()
     sum_y2.start()
-    sum_x2.start()
     for s in range(2):
         rows = slice(s * SEG_ROWS, (s + 1) * SEG_ROWS)
         low_half, back_half = halves[s]
-        adapted = dot(low_half, ga[idx[2 + s] + ACTIVE], 1, 0)
+        adapted = dot(low_half, ga[seg_block[s] + ACTIVE], 1, 0)
         po_ref[rows, :] = (acc[rows, :] + adapter_scale * adapted).astype(BF16)
-        acc[rows, :] = dot(back_half, ga[idx[2 + s]], 1, 0)
+        acc[rows, :] = dot(back_half, ga[seg_block[s]], 1, 0)
+
+    def add_group(place, side):
+        group = place * 2 + side
+        for slot, v in enumerate((own_low, own_high)):
+            hits = []
+            for s in range(2):
+                hit = ids[group * 2 + s] == v
+                if slot:
+                    hit = hit & (own_high != own_low)
+                hits.append(jnp.where(hit, 1.0, 0.0).astype(F32))
+            for du in range(2):
+                at = group * 4 + du * 2
+                asum[du * 2 + slot] += hits[0] * gb[at].astype(F32) + hits[1] * gb[at + 1].astype(F32)
+
+    def add_side(k, side):
+        for place in parts.places(k):
+            add_group(place, side)
+
+    def finish_y1():
+        sum_y1.finish()
+        for h in range(2):
+            def first_y(j, carry):
+                v = sum_y1.total(h, j).astype(BF16)
+                s2[h * hx + j, 0] = v[:RANK]
+                s2[h * hx + j, 1] = v[RANK:]
+                return carry
+
+            lax.fori_loop(0, hx, first_y, 0)
+        sum_x2.start()
+
+    def finish_frozen():
+        sum_y2.finish()
+        sum_x2.finish()
+        for s, ring in ((0, sum_y2), (1, sum_x2)):
+            for h in range(2):
+                rows = slice(s * SEG_ROWS + h * RANK, s * SEG_ROWS + (h + 1) * RANK)
+                gi_ref[rows, :] = (ring.total(h) + acc[rows, :]).astype(BF16)
+
     for k in range(max(parts.steps, sum_y2.steps)):
-        for ring in (parts, sum_y2, sum_x2):
-            if k < ring.steps:
-                ring.step(k)
-        if k == sum_y2.steps - 1:
-            sum_y2.finish()
-            sum_x2.finish()
-            for s, ring in ((0, sum_y2), (1, sum_x2)):
-                for h in range(2):
-                    rows = slice(s * SEG_ROWS + h * RANK, s * SEG_ROWS + (h + 1) * RANK)
-                    gi_ref[rows, :] = (ring.total(h) + acc[rows, :]).astype(BF16)
-    parts.finish()
-
-    segs = owners * ACTIVE
-    for base, out in ((0, dg_ref), (ACTIVE, ug_ref)):
-        def gather(i, carry):
-            g, s = lax.div(i, 2), lax.rem(i, 2)
-            block = gb[g * 4 + base + s].astype(F32)
-            return carry[0] + mask[1 + i] * block, carry[1] + mask[1 + segs + i] * block
-
-        zero = jnp.zeros((RANK, COLS), F32)
-        first, second = lax.fori_loop(0, segs, gather, (zero, zero))
-
-        def place(i, carry):
-            at = 1 + 2 * segs + i
-            out[i] = (mask[at] * first + mask[at + ADP_OWN] * second).astype(BF16)
-            return carry
-
-        lax.fori_loop(0, ADP_OWN, place, 0)
+        if k < parts.steps:
+            parts.step(k)
+        if k == 0:
+            finish_y1()
+            parts.own_copy().wait()
+            add_side(0, core)
+        for ring, j in ((sum_y2, k), (sum_x2, k - 1)):
+            if 0 <= j < ring.steps:
+                ring.step(j)
+        if k < parts.steps:
+            parts.pair_wait(k)
+            add_side(k, 1 - core)
+            add_side(k + 1, core)
+        if k == max(sum_y2.steps, sum_x2.steps + 1) - 1:
+            finish_frozen()
+    parts.pair_wait(parts.steps)
+    add_side(parts.steps, 1 - core)
+    sums_ref[...] = asum[...].astype(BF16)
 
     panels.drain()
     parts.drain()
@@ -369,6 +420,21 @@
         ring.drain()
     to_peer(others, others, 0, 1).wait_send()
     to_peer(others, others, 1, 1).wait_send()
+
+
+def place_kernel(segs, ids, po_in, gi_in, sums, po_ref, gi_ref, dg_ref, ug_ref):
+    start = lax.axis_index("adapter") * ADP_OWN
+    low, high = named_range(ids, segs, lax.axis_index("adapter"))
+    po_ref[...] = po_in[...]
+    gi_ref[...] = gi_in[...]
+    for base, out in ((0, dg_ref), (ACTIVE, ug_ref)):
+        def place(i, carry):
+            first = jnp.where(start + i == low, 1.0, 0.0).astype(F32)
+            second = jnp.where((start + i == high) & (high != low), 1.0, 0.0).astype(F32)
+            out[i] = (first * sums[base].astype(F32) + second * sums[base + 1].astype(F32)).astype(BF16)
+            return carry
+
+        lax.fori_loop(0, ADP_OWN, place, 0)
 
 
 def per_device(
@@ -382,35 +448,15 @@
     owners, tensors = lax.axis_size("adapter"), lax.axis_size("tensor")
     nz, nx = owners // 2, X_CHIPS
     ny = tensors // nx
-    me = lax.axis_index("adapter")
-    all_ids = jnp.arange(owners * ADP_OWN, dtype=jnp.int32)
-    use = jnp.any(segment_adapter[:, None] == all_ids[None, :], axis=0)
-    grid = use.reshape(owners, ADP_OWN).astype(jnp.int32)
-    rank = jnp.cumsum(grid, axis=1) - 1
-    group_ids = lax.dynamic_slice_in_dim(segment_adapter, me * 2, 2)
-    slot = jnp.sum(
-        jnp.where(group_ids[:, None] == all_ids[None, :], rank.reshape(1, -1), 0), axis=1
-    )
-    own_use = lax.dynamic_index_in_dim(grid, me, 0, keepdims=False)
-    own_rank = lax.dynamic_index_in_dim(rank, me, 0, keepdims=False)
-    picker = (own_rank[None, :] == jnp.arange(ACTIVE, dtype=jnp.int32)[:, None]) & (
-        own_use[None, :] > 0
-    )
-    own_local = jnp.sum(jnp.where(picker, jnp.arange(ADP_OWN, dtype=jnp.int32)[None, :], 0), axis=1)
-    idx = jnp.concatenate([own_local, (group_ids // ADP_OWN) * 4 + slot]).astype(jnp.int32)
-    own_named = jnp.any(picker, axis=1)
-    named = own_named[:, None] & (segment_adapter[None, :] == (me * ADP_OWN + own_local)[:, None])
-    same = (group_ids[0] == group_ids[1]).reshape(1)
-    mask = jnp.concatenate([same, named.reshape(-1), picker.reshape(-1)]).astype(F32)
-
     rows, width = rollout_activations.shape
     blocks = owners * 4
     slots_x, slots_y = chains_of(nx)[1], chains_of(ny)[1]
     vmem = pltpu.VMEM
     dma, block = pltpu.SemaphoreType.DMA, (RANK, COLS)
-    gather_sems = [dma(()), dma((2, nz // 2, 2)), dma(())]
+    gather_sems = [dma(()), dma((2, nz // 2, 2)), dma((nz // 2 + 1,))]
     seg = (SEG_ROWS, COLS)
     scratch = [
+        vmem((4,) + block, F32),
         vmem((rows, width), BF16),
         vmem((tensors, COLS, COLS), BF16),
         vmem((rows, COLS), F32),
@@ -443,31 +489,32 @@
         pl.BlockSpec(memory_space=pltpu.VMEM),
         pl.BlockSpec(memory_space=pl.ANY),
     )
-    out = [
-        jax.ShapeDtypeStruct((rows, COLS), BF16),
-        jax.ShapeDtypeStruct((rows, COLS), BF16),
-        jax.ShapeDtypeStruct((ADP_OWN,) + block, BF16),
-        jax.ShapeDtypeStruct((ADP_OWN,) + block, BF16),
-    ]
+    like_rows = jax.ShapeDtypeStruct((rows, COLS), BF16)
+    like_panels = jax.ShapeDtypeStruct((ADP_OWN,) + block, BF16)
+    po, gi, sums = pl.pallas_call(
+        functools.partial(step_kernel, owners, tensors),
+        out_shape=[like_rows, like_rows, jax.ShapeDtypeStruct((4,) + block, BF16)],
+        in_specs=[smem, any_space, any_space, whole, whole, whole],
+        out_specs=[whole] * 3,
+        scratch_shapes=scratch,
+        compiler_params=pltpu.CompilerParams(
+            collective_id=0, has_side_effects=True, vmem_limit_bytes=60 * 1024 * 1024
+        ),
+    )(
+        segment_adapter,
+        rollout_activations,
+        projection_weight.reshape(tensors, COLS, COLS),
+        adapter_down_panels,
+        adapter_up_panels,
+        output_gradient,
+    )
     return tuple(
         pl.pallas_call(
-            functools.partial(step_kernel, owners, tensors),
-            out_shape=out,
-            in_specs=[smem, smem, any_space, any_space, whole, whole, whole],
+            functools.partial(place_kernel, owners * 2),
+            out_shape=[like_rows, like_rows, like_panels, like_panels],
+            in_specs=[smem, whole, whole, whole],
             out_specs=[whole] * 4,
-            scratch_shapes=scratch,
-            compiler_params=pltpu.CompilerParams(
-                collective_id=0, has_side_effects=True, vmem_limit_bytes=60 * 1024 * 1024
-            ),
-        )(
-            idx,
-            mask,
-            rollout_activations,
-            projection_weight.reshape(tensors, COLS, COLS),
-            adapter_down_panels,
-            adapter_up_panels,
-            output_gradient,
-        )
+        )(segment_adapter, po, gi, sums)
     )
 
 

time: 116 us -> 96.3 us (0.83)
  local copies, waits for them, and re-layouts: 8.55 us -> 0 us
  Pallas kernels: 101 us -> 95.3 us
  other arithmetic: 4.06 us -> 0 us
  between operations: 1.97 us -> 0.64 us
    pallas_call x1, Pallas kernels: 101 us -> 92.3 us  [per_device(): pl.pallas_call(functools.partial(step_kernel, owners, tensors), out_shape...]
    unnamed x4 -> x0, local copies, waits for them, and re-layouts: 6.9 us -> none
    pallas_call x0 -> x1, Pallas kernels: none -> 3.01 us  [per_device(): pl.pallas_call(functools.partial(place_kernel, owners * 2), out_shape=[li...]
where the time goes in v2:
time: 96.3 us; the launch traced here: 96 us
  Pallas kernels  95.3 us (99%)
    pallas_call x1, Pallas kernels, per_device(): pl.pallas_call(functools.partial(step_kernel, owners, tensors), out_shape...  92.3 us
    pallas_call x1, Pallas kernels, per_device(): pl.pallas_call(functools.partial(place_kernel, owners * 2), out_shape=[li...  3.01 us

profile of v2, /device:TPU:1, one launch (start us, length us, event | category | flops | bytes accessed | tf_op | source)
XLA Modules:
  0.0 96.0 jit_solution(11723216971605115453)
XLA Ops:
  0.6 92.3 %shard_map.93 = (bf16[256,256]{1,0:T(8,128)(2,1)}, bf16[256,256]{1,0:T(8,128)(2,1)}, bf16[4,64,256]{2,1,0:T(8,128)(2,1)}) custom-call(s32[48]{0:T(128)} %ids.3, bf16[256,8192]{1,0:T(8,128)(2,1)} %x_hbm.1, bf16[32,256,256]{2,1,0:T(8,128)(2,1)} %bitcast.1, bf16[16,64,256]{2,1,0:T(8,128)(2,1)} %down_ref.1, bf16[16,64,256]{2,1,0:T(8,128)(2,1)} %up_ref.1, ...), custom_call_target="tpu_custom_call" | custom-call | tf_op jit(solution)/shard_map/pallas_call | solution.py:494
  92.9 3.0 %shard_map.94 = (bf16[256,256]{1,0:T(8,128)(2,1)}, bf16[256,256]{1,0:T(8,128)(2,1)}, bf16[16,64,256]{2,1,0:T(8,128)(2,1)}, bf16[16,64,256]{2,1,0:T(8,128)(2,1)}) custom-call(s32[48]{0:T(128)} %ids.3, bf16[256,256]{1,0:T(8,128)(2,1)} %get-tuple-element.7.po_in, bf16[256,256]{1,0:T(8,128)(2,1)} %get-tuple-element.8.gi_in, ...), custom_call_target="tpu_custom_call" | custom-call | tf_op jit(solution)/shard_map/pallas_call | solution.py:512

commit v3 on v2

--- a/solution.py
+++ b/solution.py
@@ -115,10 +115,10 @@
         self.steps = n // 2
 
     def has(self, d, k, ch):
-        return k < self.steps - 1 or (k == self.steps - 1 and d == ch)
-
-    def rows(self, z, core, ch):
-        return self.out.at[pl.ds((z * 2 + core) * 4 + ch * 2, 2)]
+        return k < self.steps - 1 or (k == self.steps - 1 and d == ch // 2)
+
+    def rows(self, z, core, ch, count=1):
+        return self.out.at[pl.ds((z * 2 + core) * 4 + ch, count)]
 
     def ring(self, src, dst, d, k, ch):
         sign = 1 - 2 * d
@@ -148,32 +148,32 @@
         )
 
     def start(self):
-        for ch in range(2):
-            src, dst = self.own.at[pl.ds(ch * 2, 2)], self.rows(self.z, self.core, ch)
+        for ch in range(4):
+            src, dst = self.own.at[pl.ds(ch, 1)], self.rows(self.z, self.core, ch)
             for d in range(2):
                 if self.has(d, 0, ch):
                     self.ring(src, dst, d, 0, ch).start()
-        for ch in range(2):
-            src, dst = self.own.at[pl.ds(ch * 2, 2)], self.rows(self.z, self.core, ch)
-            self.pair(src, dst, 0).start()
+        self.pair(self.own, self.rows(self.z, self.core, 0, 4), 0).start()
         self.own_copy().start()
 
     def step(self, k):
-        for ch in range(2):
+        z_from = [lax.rem(self.z - sign * (k + 1) + 2 * self.n, self.n) for sign in (1, -1)]
+        for ch in range(4):
             for d in range(2):
                 if not self.has(d, k, ch):
                     continue
-                sign = 1 - 2 * d
-                z_from = lax.rem(self.z - sign * (k + 1) + 2 * self.n, self.n)
-                block = self.rows(z_from, self.core, ch)
+                block = self.rows(z_from[d], self.core, ch)
                 self.ring(block, block, d, k, ch).wait_recv()
                 if self.has(d, k + 1, ch):
                     self.ring(block, block, d, k + 1, ch).start()
-                self.pair(block, block, k + 1).start()
+        for d in range(2):
+            chunks = [ch for ch in range(4) if self.has(d, k, ch)]
+            block = self.rows(z_from[d], self.core, chunks[0], len(chunks))
+            self.pair(block, block, k + 1).start()
 
     def pair_wait(self, k):
-        count = 2 if k == 0 else sum(self.has(d, k - 1, ch) for d in range(2) for ch in range(2))
-        landed = self.out.at[pl.ds(0, 2 * count)]
+        count = 4 if k == 0 else sum(self.has(d, k - 1, ch) for d in range(2) for ch in range(4))
+        landed = self.out.at[pl.ds(0, count)]
         self.pair(landed, landed, k).wait_recv()
 
     def places(self, k):
@@ -246,6 +246,8 @@
     sum_y2 = RingSum(ny, y, along_y, s1, q1, s_q1, v_q1)
     sum_x2 = RingSum(nx, x, along_x, s2, q2, s_q2, v_q2)
 
+    pl.semaphore_wait(barrier, tensors + 2)
+    panels.start()
     w_in.wait()
 
     def frozen_term(t, carry):
@@ -255,9 +257,9 @@
         f2[ty, lax.div(tx, hx), lax.rem(tx, hx)] = term[SEG_ROWS:]
         return carry
 
-    lax.fori_loop(0, tensors, frozen_term, 0)
-    pl.semaphore_wait(barrier, tensors + 2)
-    panels.start()
+    lax.fori_loop(0, tensors // 2, frozen_term, 0)
+    panels.step(0)
+    lax.fori_loop(tensors // 2, tensors, frozen_term, 0)
     sum_x1.start()
     sum_y1.start()
     seg_block = []
@@ -268,7 +270,7 @@
         seg_block.append(owner * 4 + jnp.where(v > low, 1, 0))
     same = jnp.where(ids[me_a * 2] == ids[me_a * 2 + 1], 1.0, 0.0).astype(F32)
     asum[...] = jnp.zeros_like(asum)
-    order = [(panels, 0), (panels, 1), (sum_y1, 0), (sum_x1, 0), (panels, 2), (panels, 3), (panels, 4), (sum_y1, 1)]
+    order = [(panels, 1), (panels, 2), (sum_y1, 0), (sum_x1, 0), (panels, 3), (panels, 4), (sum_y1, 1)]
     order += [(panels, k) for k in range(5, panels.steps)]
     for ring, k in order:
         if k < ring.steps:
@@ -453,7 +455,7 @@
     slots_x, slots_y = chains_of(nx)[1], chains_of(ny)[1]
     vmem = pltpu.VMEM
     dma, block = pltpu.SemaphoreType.DMA, (RANK, COLS)
-    gather_sems = [dma(()), dma((2, nz // 2, 2)), dma((nz // 2 + 1,))]
+    gather_sems = [dma(()), dma((2, nz // 2, 4)), dma((nz // 2 + 1,))]
     seg = (SEG_ROWS, COLS)
     scratch = [
         vmem((4,) + block, F32),

time: 96.3 us -> 91.9 us (0.954)
  Pallas kernels: 95.3 us -> 91.1 us
    pallas_call x1, Pallas kernels: 92.3 us -> 88 us  [per_device(): pl.pallas_call(functools.partial(step_kernel, owners, tensors), out_shape...]
where the time goes in v3:
time: 91.9 us; the launch traced here: 91.7 us
  Pallas kernels  91.1 us (99%)
    pallas_call x1, Pallas kernels, per_device(): pl.pallas_call(functools.partial(step_kernel, owners, tensors), out_shape...  88 us
    pallas_call x1, Pallas kernels, per_device(): pl.pallas_call(functools.partial(place_kernel, owners * 2), out_shape=[li...  3.01 us

profile of v3, /device:TPU:1, one launch (start us, length us, event | category | flops | bytes accessed | tf_op | source)
XLA Modules:
  0.0 91.7 jit_solution(3431623952191746369)
XLA Ops:
  0.6 88.0 %shard_map.93 = (bf16[256,256]{1,0:T(8,128)(2,1)}, bf16[256,256]{1,0:T(8,128)(2,1)}, bf16[4,64,256]{2,1,0:T(8,128)(2,1)}) custom-call(s32[48]{0:T(128)} %ids.3, bf16[256,8192]{1,0:T(8,128)(2,1)} %x_hbm.1, bf16[32,256,256]{2,1,0:T(8,128)(2,1)} %bitcast.1, bf16[16,64,256]{2,1,0:T(8,128)(2,1)} %down_ref.1, bf16[16,64,256]{2,1,0:T(8,128)(2,1)} %up_ref.1, ...), custom_call_target="tpu_custom_call" | custom-call | tf_op jit(solution)/shard_map/pallas_call | solution.py:496
  88.7 3.0 %shard_map.94 = (bf16[256,256]{1,0:T(8,128)(2,1)}, bf16[256,256]{1,0:T(8,128)(2,1)}, bf16[16,64,256]{2,1,0:T(8,128)(2,1)}, bf16[16,64,256]{2,1,0:T(8,128)(2,1)}) custom-call(s32[48]{0:T(128)} %ids.3, bf16[256,256]{1,0:T(8,128)(2,1)} %get-tuple-element.7.po_in, bf16[256,256]{1,0:T(8,128)(2,1)} %get-tuple-element.8.gi_in, ...), custom_call_target="tpu_custom_call" | custom-call | tf_op jit(solution)/shard_map/pallas_call | solution.py:514

commit v4 on v3

--- a/solution.py
+++ b/solution.py
@@ -207,7 +207,7 @@
     po_ref, gi_ref, sums_ref,
     asum, xv, wv, acc, pk, ga, gk, gb, f1, f2, r1, r2, s1, s2, q1, q2, part, inbox, mine, total,
     in_sem, own_sem, gs_a, gr_a, gp_a, gs_b, gr_b, gp_b,
-    s_r1, v_r1, s_r2, v_r2, s_q1, v_q1, s_q2, v_q2, ar_send, ar_recv,
+    s_r1, v_r1, s_r2, v_r2, s_q1, v_q1, s_q2, v_q2, ar_send, ar_recv, told,
 ):
     nz, nx = owners // 2, X_CHIPS
     ny = tensors // nx
@@ -219,13 +219,22 @@
     barrier = pltpu.get_barrier_semaphore()
     for to in (lax.rem(z + 1, nz) * 2 + core, lax.rem(z + nz - 1, nz) * 2 + core, z * 2 + 1 - core):
         pl.semaphore_signal(barrier, inc=1, device_id={"adapter": to}, device_id_type=MESH)
-
-    def greet(d, carry):
-        to = lax.rem(me_t + d, tensors)
+    x_sides = [y * nx + lax.rem(x + 1, nx), y * nx + lax.rem(x + nx - 1, nx)]
+    y_sides = [lax.rem(y + 1, ny) * nx + x, lax.rem(y + ny - 1, ny) * nx + x]
+    for to in x_sides + y_sides:
         pl.semaphore_signal(barrier, inc=1, device_id={"tensor": to}, device_id_type=MESH)
-        return carry
-
-    lax.fori_loop(1, tensors, greet, 0)
+    rounds = [y_sides] * (ny // 2 - 1) + [x_sides] * (nx // 2)
+
+    def tell(k):
+        if k < len(rounds):
+            for to in rounds[k]:
+                pl.semaphore_signal(told.at[k], inc=1, device_id={"tensor": to}, device_id_type=MESH)
+
+    def hear(k):
+        if k < len(rounds):
+            pl.semaphore_wait(told.at[k], 2)
+            tell(k + 1)
+
     w_in = pltpu.make_async_copy(w_hbm, wv, in_sem.at[0])
     x_in = pltpu.make_async_copy(x_hbm, xv, in_sem.at[1])
     w_in.start()
@@ -246,8 +255,9 @@
     sum_y2 = RingSum(ny, y, along_y, s1, q1, s_q1, v_q1)
     sum_x2 = RingSum(nx, x, along_x, s2, q2, s_q2, v_q2)
 
-    pl.semaphore_wait(barrier, tensors + 2)
+    pl.semaphore_wait(barrier, 7)
     panels.start()
+    tell(0)
     w_in.wait()
 
     def frozen_term(t, carry):
@@ -259,6 +269,7 @@
 
     lax.fori_loop(0, tensors // 2, frozen_term, 0)
     panels.step(0)
+    hear(0)
     lax.fori_loop(tensors // 2, tensors, frozen_term, 0)
     sum_x1.start()
     sum_y1.start()
@@ -275,6 +286,10 @@
     for ring, k in order:
         if k < ring.steps:
             ring.step(k)
+        if ring is panels:
+            hear(k)
+    for k in range(panels.steps, len(rounds)):
+        hear(k)
     panels.own_copy().wait()
     for k in range(panels.steps + 1):
         panels.pair_wait(k)
@@ -289,17 +304,20 @@
         per = tensors // 2
         part[s * per:(s + 1) * per] = both.reshape(per, SEG_ROWS // per, 2 * RANK)
 
-    def to_peer(src, dst, phase, d):
+    peers = [(dy, dx) for dy in range(ny) for dx in range(nx) if dy or dx]
+    peers.sort(key=lambda p: (-min(p[0], ny - p[0]) - min(p[1], nx - p[1]), p))
+
+    def place_of(peer):
+        return lax.rem(y + peer[0], ny) * nx + lax.rem(x + peer[1], nx)
+
+    def to_peer(src, dst, phase, peer):
         return pltpu.make_async_remote_copy(
             src_ref=src, dst_ref=dst, send_sem=ar_send.at[phase], recv_sem=ar_recv.at[phase],
-            device_id={"tensor": lax.rem(me_t + d, tensors)}, device_id_type=MESH,
+            device_id={"tensor": place_of(peer)}, device_id_type=MESH,
         )
 
-    def scatter(d, carry):
-        to_peer(part.at[lax.rem(me_t + d, tensors)], inbox.at[d - 1], 0, d).start()
-        return carry
-
-    lax.fori_loop(1, tensors, scatter, 0)
+    for i, peer in enumerate(peers):
+        to_peer(part.at[place_of(peer)], inbox.at[i], 0, peer).start()
 
     acc[...] = jnp.zeros_like(acc)
 
@@ -311,18 +329,15 @@
     lax.fori_loop(0, tensors, forward, 0)
 
     others = inbox.at[pl.ds(0, tensors - 1)]
-    to_peer(others, others, 0, 1).wait_recv()
+    to_peer(others, others, 0, peers[-1]).wait_recv()
     value = part[me_t]
     for d in range(tensors - 1):
         value = value + inbox[d]
     mine[...] = value
     total[me_t] = value
 
-    def spread(d, carry):
-        to_peer(mine, total.at[me_t], 1, d).start()
-        return carry
-
-    lax.fori_loop(1, tensors, spread, 0)
+    for peer in peers:
+        to_peer(mine, total.at[me_t], 1, peer).start()
 
     for k in range(2, sum_y1.steps):
         sum_y1.step(k)
@@ -336,7 +351,7 @@
 
         lax.fori_loop(0, hy, first_x, 0)
     rest = total.at[pl.ds(0, tensors - 1)]
-    to_peer(rest, rest, 1, 1).wait_recv()
+    to_peer(rest, rest, 1, peers[-1]).wait_recv()
 
     ranks = total[...].reshape(2 * SEG_ROWS, 2 * RANK)
     halves, downs, ups = [], [], []
@@ -420,8 +435,8 @@
     parts.drain()
     for ring in (sum_x1, sum_y1, sum_y2, sum_x2):
         ring.drain()
-    to_peer(others, others, 0, 1).wait_send()
-    to_peer(others, others, 1, 1).wait_send()
+    to_peer(others, others, 0, peers[-1]).wait_send()
+    to_peer(others, others, 1, peers[-1]).wait_send()
 
 
 def place_kernel(segs, ids, po_in, gi_in, sums, po_ref, gi_ref, dg_ref, ug_ref):
@@ -431,9 +446,8 @@
     gi_ref[...] = gi_in[...]
     for base, out in ((0, dg_ref), (ACTIVE, ug_ref)):
         def place(i, carry):
-            first = jnp.where(start + i == low, 1.0, 0.0).astype(F32)
-            second = jnp.where((start + i == high) & (high != low), 1.0, 0.0).astype(F32)
-            out[i] = (first * sums[base].astype(F32) + second * sums[base + 1].astype(F32)).astype(BF16)
+            other = jnp.where(start + i == high, sums[base + 1], jnp.zeros((RANK, COLS), BF16))
+            out[i] = jnp.where(start + i == low, sums[base], other)
             return carry
 
         lax.fori_loop(0, ADP_OWN, place, 0)
@@ -485,7 +499,7 @@
     ]
     for slots in (slots_x, slots_y, slots_y, slots_x):
         scratch += [dma(()), dma((slots,))]
-    scratch += [dma((2,)), dma((2,))]
+    scratch += [dma((2,)), dma((2,)), pltpu.SemaphoreType.REGULAR((ny // 2 - 1 + nx // 2,))]
     smem, whole, any_space = (
         pl.BlockSpec(memory_space=pltpu.SMEM),
         pl.BlockSpec(memory_space=pltpu.VMEM),

time: 91.9 us -> 87 us (0.947)
  Pallas kernels: 91.1 us -> 86.2 us
    pallas_call x1, Pallas kernels: 88 us -> 83.4 us  [per_device(): pl.pallas_call(functools.partial(step_kernel, owners, tensors), out_shape...]
where the time goes in v4:
time: 87 us; the launch traced here: 86.8 us
  Pallas kernels  86.2 us (99%)
    pallas_call x1, Pallas kernels, per_device(): pl.pallas_call(functools.partial(step_kernel, owners, tensors), out_shape...  83.4 us
    pallas_call x1, Pallas kernels, per_device(): pl.pallas_call(functools.partial(place_kernel, owners * 2), out_shape=[li...  2.78 us

profile of v4, /device:TPU:1, one launch (start us, length us, event | category | flops | bytes accessed | tf_op | source)
XLA Modules:
  0.0 86.8 jit_solution(5986359861676225023)
XLA Ops:
  0.6 83.4 %shard_map.93 = (bf16[256,256]{1,0:T(8,128)(2,1)}, bf16[256,256]{1,0:T(8,128)(2,1)}, bf16[4,64,256]{2,1,0:T(8,128)(2,1)}) custom-call(s32[48]{0:T(128)} %ids.3, bf16[256,8192]{1,0:T(8,128)(2,1)} %x_hbm.1, bf16[32,256,256]{2,1,0:T(8,128)(2,1)} %bitcast.1, bf16[16,64,256]{2,1,0:T(8,128)(2,1)} %down_ref.1, bf16[16,64,256]{2,1,0:T(8,128)(2,1)} %up_ref.1, ...), custom_call_target="tpu_custom_call" | custom-call | tf_op jit(solution)/shard_map/pallas_call | solution.py:510
  84.0 2.8 %shard_map.94 = (bf16[256,256]{1,0:T(8,128)(2,1)}, bf16[256,256]{1,0:T(8,128)(2,1)}, bf16[16,64,256]{2,1,0:T(8,128)(2,1)}, bf16[16,64,256]{2,1,0:T(8,128)(2,1)}) custom-call(s32[48]{0:T(128)} %ids.3, bf16[256,256]{1,0:T(8,128)(2,1)} %get-tuple-element.7.po_in, bf16[256,256]{1,0:T(8,128)(2,1)} %get-tuple-element.8.gi_in, ...), custom_call_target="tpu_custom_call" | custom-call | tf_op jit(solution)/shard_map/pallas_call | solution.py:528
